TPU v7x, 256 devices: a whole 4x4x8 slice. The times are simulated.
256 devices in a mesh: ket: 16 (over x, y_hi, core), bra: 16 (over z, y_lo).
Axes of the slice: x: 4, y: 4 (y_hi: 2, y_lo: 2; y = y_hi * 2 + y_lo), z: 8, core: 2. Of those that a mesh axis runs over, the one named last changes fastest.
Arguments:
- density: bfloat16 [2, 2, 12288, 12288], P(None, None, 'ket', 'bra'), may hold values from -6 to 6
- coupling: bfloat16 [48, 3, 256, 256], P('bra'), may hold values from -0.21875 to 0.21875
- block_cols: int32 [48, 3], replicated, may hold values from 0 to 47, as said below
- block_count: int32 [48], replicated, may hold values from 2 to 3, as said below
- energies: float32 [12288], replicated, may hold values from -0.5 to 97
Outputs:
- dissipated: bfloat16 [2, 2, 12288, 12288], P(None, None, 'ket', 'bra')
Inputs may be any that keep to these rules, and one draw needn't show every extreme that they name: Row i of block_cols holds i - 1, i and i + 1 in some order; entries that would lie outside 0 to 47 stand last and are replaced by i. Slots k < block_count[i] name distinct blocks. block_count[i] is at most the number of block columns of i - 1, i, i + 1 inside the grid.
All inputs are finite; a program needn't handle non-finite values.
Results may differ from a plain program's by a relative error of at most 0.0054.
Values may be sent and summed in bfloat16 or wider, within the bound.
A program may use at most 320 MiB of HBM per device.

v0:
```python
import jax
import jax.numpy as jnp
from jax import lax
from jax.sharding import PartitionSpec as P

thermal_beta_factor = 1.0
frequency_cutoff_scale = 4.0


def broadcast(value, axis, source):
    kept = jnp.where(lax.axis_index(axis) == source, value, 0).astype(value.dtype)
    return lax.psum(kept, axis)


def with_halo(block, sides, width):
    for axis, dim in sides:
        count = lax.axis_size(axis)
        forward = [(i, i + 1) for i in range(count - 1)]
        backward = [(target, source) for source, target in forward]
        low = lax.ppermute(
            lax.slice_in_dim(block, block.shape[dim] - width, None, axis=dim), axis, forward
        )
        high = lax.ppermute(lax.slice_in_dim(block, 0, width, axis=dim), axis, backward)
        block = jnp.concatenate([low, block, high], axis=dim)
    return block


def weigh(matrix, start_block, block_cols, block_count, energies):
    row_count = matrix.shape[0]
    slots = matrix.shape[1]
    block_size = matrix.shape[2]
    block_total = block_cols.shape[0]
    position = start_block + jnp.arange(row_count, dtype=jnp.int32)
    inside = (position >= 0) & (position < block_total)
    clamped = jnp.clip(position, 0, block_total - 1)
    columns = jnp.take(block_cols, clamped, axis=0)
    counts = jnp.take(block_count, clamped, axis=0)
    kept_levels = (jnp.arange(slots, dtype=jnp.int32)[None, :] < counts[:, None]) & inside[:, None]
    levels = energies.reshape(block_total, block_size)
    row_levels = jnp.take(levels, clamped, axis=0)
    col_levels = jnp.take(levels, columns.reshape(-1), axis=0).reshape(row_count, slots, block_size)
    energy_detuning = row_levels[:, None, :, None] - col_levels[:, :, None, :]
    spectral_density = jax.nn.sigmoid(thermal_beta_factor * energy_detuning) * jnp.exp(
        -jnp.abs(energy_detuning) / frequency_cutoff_scale
    )
    held = kept_levels[:, :, None, None]
    operator = jnp.where(held, matrix, jnp.zeros_like(matrix))
    weighted = jnp.where(
        held, matrix.astype(jnp.float32) * spectral_density, jnp.float32(0.0)
    ).astype(jnp.bfloat16)
    return (operator, weighted, columns)


def left_apply(matrix, columns, start_block, source_operator):
    copies, halves, source_rows, breadth = source_operator.shape
    row_count, slots, block_size = (matrix.shape[0], matrix.shape[1], matrix.shape[2])
    pieces = source_operator.reshape(copies, halves, source_rows // block_size, block_size, breadth)
    relative = (columns - start_block).reshape(-1)
    picked = jnp.take(pieces, relative, axis=2).reshape(
        copies, halves, row_count, slots, block_size, breadth
    )
    result = jnp.einsum("ikab,rpikbc->rpiac", matrix, picked, preferred_element_type=jnp.float32)
    return result.reshape(copies, halves, row_count * block_size, breadth)


def right_apply(matrix, columns, start_block, source_operator):
    copies, halves, source_rows, breadth = source_operator.shape
    row_count, slots, block_size = (matrix.shape[0], matrix.shape[1], matrix.shape[2])
    pieces = source_operator.reshape(copies, halves, source_rows, breadth // block_size, block_size)
    relative = (columns - start_block).reshape(-1)
    picked = jnp.take(pieces, relative, axis=3).reshape(
        copies, halves, source_rows, row_count, slots, block_size
    )
    result = jnp.einsum("rpxjkb,jkab->rpxja", picked, matrix, preferred_element_type=jnp.float32)
    return result.reshape(copies, halves, source_rows, row_count * block_size)


def body(density, coupling, block_cols, block_count, energies):
    block_size = coupling.shape[2]
    tile_rows = density.shape[2]
    tile_cols = density.shape[3]
    row_blocks = tile_rows // block_size
    col_blocks = tile_cols // block_size
    ket_index = lax.axis_index("ket")
    bra_index = lax.axis_index("bra")
    panel_owner = ket_index * lax.axis_size("bra") // lax.axis_size("ket")
    panel = broadcast(coupling, "bra", panel_owner)
    row_start = ket_index * row_blocks
    col_start = bra_index * col_blocks
    bordered = with_halo(density, (("ket", 2), ("bra", 3)), block_size)
    row_operator, row_weighted, row_columns = weigh(
        panel, row_start, block_cols, block_count, energies
    )
    col_operator, col_weighted, col_columns = weigh(
        coupling, col_start, block_cols, block_count, energies
    )
    commutand = (
        left_apply(
            row_weighted,
            row_columns,
            row_start - 1,
            bordered[:, :, :, block_size : block_size + tile_cols],
        )
        - right_apply(
            col_weighted,
            col_columns,
            col_start - 1,
            bordered[:, :, block_size : block_size + tile_rows, :],
        )
    ).astype(jnp.bfloat16)
    outer = with_halo(commutand, (("ket", 2), ("bra", 3)), block_size)
    dissipated = (
        right_apply(
            col_operator,
            col_columns,
            col_start - 1,
            outer[:, :, block_size : block_size + tile_rows, :],
        )
        - left_apply(
            row_operator,
            row_columns,
            row_start - 1,
            outer[:, :, :, block_size : block_size + tile_cols],
        )
    ).astype(jnp.bfloat16)
    return dissipated


def solution(mesh):
    return jax.shard_map(
        body,
        mesh=mesh,
        in_specs=(P(None, None, "ket", "bra"), P("bra", None, None, None), P(), P(), P()),
        out_specs=P(None, None, "ket", "bra"),
        check_vma=False,
    )
```

profile of v0, /device:TPU:92, one launch (start us, length us, event | category | flops | bytes accessed | tf_op | source)
XLA Modules:
  0.0 556.6 jit_solution(13479946788003193734)
XLA Ops:
  7.7 3.8 fusion.59
  11.5 2.6 collective-permute-start.1
  14.1 1.9 collective-permute-start
  22.0 84.1 %collective-permute-done = bf16[2,2,256,768]{3,2,1,0:T(8,128)(2,1)} collective-permute-done((bf16[2,2,256,768]{3,2,1,0:T(8,128)(2,1)}, bf16[2,2,256,768]{3,2,1,0:T(8,128)(2,1)}, u32[]{:S(2)}, u32[]{:S(2)}) %collective-permute-start) | collective-permute-done | bytes 1572896 | tf_op jit(solution)/shard_map/ppermute | solution.py:20
  106.1 1.5 constant_dynamic-update-slice_fusion.2
  107.7 2.7 constant_dynamic-update-slice_fusion.1
  110.5 2.9 fusion.57
  113.4 3.4 collective-permute-start.2
  116.8 3.4 collective-permute-start.3
  120.2 3.7 copy.31
  123.8 10.0 %gather_fusion.2 = bf16[9,2,2,256,768]{4,3,2,1,0:T(8,128)(2,1)} fusion(bf16[2,2,5,256,768]{4,3,1,0,2:T(8,128)(2,1)} %copy.31, s32[1024]{0:T(1024)S(1)} %get-tuple-element.25), kind=kCustom, calls=%fused_computation.2.clone | custom fusion | bytes 28311588 | tf_op jit(solution)/shard_map/jit(_take)/gather | solution.py:59
  133.9 10.7 %broadcast_select_fusion.3 = bf16[9,2,2,256,768]{4,3,2,1,0:T(8,128)(2,1)} fusion(bf16[9,2,2,256,768]{4,3,2,1,0:T(8,128)(2,1)} %gather_fusion.2, pred[9]{0:T(512)(128)(4,1)S(1)} %compare_and_fusion.3), kind=kLoop, calls=%fused_computation.15 | loop fusion | flops 7077888 | bytes 28311560 | tf_op jit(solution)/shard_map/jit(_take)/select_n | solution.py:59
  144.6 84.9 %all-reduce.2.cloned.1.call-done = bf16[3,3,256,256]{3,2,1,0:T(8,128)(2,1)} async-done(((bf16[3,3,256,256]{3,2,1,0:T(8,128)(2,1)}), bf16[3,3,256,256]{3,2,1,0:T(8,128)(2,1)}) %all-reduce.2.cloned.1.call-update) | async-done | bytes 1179664 | tf_op jit(solution)/shard_map/psum | solution.py:12
  229.5 9.1 %convolution_bitcast_fusion.3 = f32[2,2,3,256,768]{4,3,1,0,2:T(8,128)S(1)} fusion(bf16[2,2,3,3,256,768]{5,4,1,0,3,2:T(8,128)(2,1)} %bitcast.92, bf16[3,3,256,256]{3,2,1,0:T(8,128)(2,1)} %all-reduce.2.cloned.1.call-done, f32[3,3,256]{2,1,0:T(4,128)S(1)} %sub.69, f32[3,256]{1,0:T(4,128)S(1)} %broadcast_select_fusion.8, pred[3,3]{1,0:T(4,128)(4,1)S(1)} %fusion.47), kind=kOutput, calls=%fused_computation.30 | convolution fusion | flops 3630956544 | bytes 24784904 | tf_op jit(solution)/shard_map/ikab,rpikbc->rpiac/dot_general | solution.py:62
  238.6 4.8 copy.34
  243.4 6.7 %pad_maximum_fusion.4 = bf16[2,2,768,1280]{3,2,1,0:T(8,128)(2,1)} fusion(bf16[2,2,1280,256]{3,2,1,0:T(8,128)(2,1)} %collective-permute-done.3, bf16[2,2,1280,768]{3,2,1,0:T(8,128)(2,1)} %copy-done.3, bf16[2,2,1280,256]{3,2,1,0:T(8,128)(2,1)} %collective-permute-done.2), kind=kLoop, calls=%fused_computation.24 | loop fusion | flops 23592960 | bytes 20971520 | tf_op jit(solution)/shard_map/concatenate | solution.py:24
  250.1 10.7 %copy.35 = bf16[2,2,768,1280]{2,3,1,0:T(8,128)(2,1)} copy(bf16[2,2,768,1280]{3,2,1,0:T(8,128)(2,1)} %pad_maximum_fusion.4) | data formatting | bytes 15728640 | tf_op jit(solution)/shard_map/slice | solution.py:108
  260.7 7.1 %copy.36 = bf16[2,2,768,5,256]{2,4,1,0,3:T(8,128)(2,1)} copy(bf16[2,2,768,5,256]{2,4,3,1,0:T(8,128)(2,1)} %bitcast.90) | data formatting | bytes 15728640 | tf_op jit(solution)/shard_map/reshape | solution.py:69
  267.8 10.0 %gather_fusion.9 = bf16[9,2,2,768,256]{3,4,2,1,0:T(8,128)(2,1)} fusion(bf16[2,2,768,5,256]{2,4,1,0,3:T(8,128)(2,1)} %copy.36, s32[1024]{0:T(1024)S(1)} %pad_clamp_fusion), kind=kCustom, calls=%fused_computation.5.clone | custom fusion | bytes 28311588 | tf_op jit(solution)/shard_map/jit(_take)/gather | solution.py:71
  277.8 7.1 %broadcast_select_fusion = bf16[9,2,2,768,256]{3,4,2,1,0:T(8,128)(2,1)S(1)} fusion(bf16[9,2,2,768,256]{3,4,2,1,0:T(8,128)(2,1)} %gather_fusion.9, pred[9]{0:T(512)(128)(4,1)S(1)} %compare_and_fusion), kind=kLoop, calls=%fused_computation.12 | loop fusion | flops 7077888 | bytes 28311560 | tf_op jit(solution)/shard_map/jit(_take)/select_n | solution.py:71
  284.9 4.5 convolution_bitcast_fusion.2
  289.4 4.7 copy.39
  294.1 9.7 %copy.40 = f32[2,2,768,768]{3,2,1,0:T(8,128)} copy(f32[2,2,768,768]{2,3,1,0:T(8,128)} %bitcast.88) | data formatting | bytes 18874368 | tf_op jit(solution)/shard_map/reshape | solution.py:75
  303.8 10.1 %fusion.1 = bf16[2,2,768,768]{3,2,1,0:T(8,128)(2,1)} fusion(f32[2,2,768,768]{3,2,1,0:T(8,128)} %copy.40, f32[2,2,3,256,768]{4,3,2,1,0:T(8,128)} %copy.34), kind=kLoop, calls=%fused_computation.19 | loop fusion | flops 4718592 | bytes 23592960 | tf_op jit(solution)/shard_map/convert_element_type | solution.py:110
  313.9 2.2 fusion.58
  316.2 2.1 collective-permute-start.4
  318.2 5.1 collective-permute-start.5
  323.4 89.9 %collective-permute-done.4 = bf16[2,2,256,768]{3,2,1,0:T(8,128)(2,1)S(1)} collective-permute-done((bf16[2,2,256,768]{3,2,1,0:T(8,128)(2,1)S(1)}, bf16[2,2,256,768]{3,2,1,0:T(8,128)(2,1)S(1)}, u32[]{:S(2)}, u32[]{:S(2)}) %collective-permute-start.4) | collective-permute-done | bytes 1572896 | tf_op jit(solution)/shard_map/ppermute | solution.py:20
  413.3 1.1 copy-done.5
  415.0 3.1 copy-done.2
  418.1 2.6 fusion.56
  420.7 1.9 collective-permute-start.6
  422.7 3.9 collective-permute-start.7
  426.6 10.0 %gather_fusion.11 = bf16[9,2,2,256,768]{4,3,2,1,0:T(8,128)(2,1)} fusion(bf16[2,2,5,256,768]{4,3,2,1,0:T(8,128)(2,1)} %bitcast.86, s32[1024]{0:T(1024)S(1)} %get-tuple-element.25), kind=kCustom, calls=%fused_computation.8.clone | custom fusion | bytes 28311588 | tf_op jit(solution)/shard_map/jit(_take)/gather | solution.py:59
  436.6 7.0 %broadcast_select_fusion.2 = bf16[9,2,2,256,768]{4,3,2,1,0:T(8,128)(2,1)S(1)} fusion(bf16[9,2,2,256,768]{4,3,2,1,0:T(8,128)(2,1)} %gather_fusion.11, pred[9]{0:T(512)(128)(4,1)S(1)} %compare_and_fusion.3), kind=kLoop, calls=%fused_computation.14 | loop fusion | flops 7077888 | bytes 28311560 | tf_op jit(solution)/shard_map/jit(_take)/select_n | solution.py:59
  443.6 5.2 convolution_bitcast_fusion
  448.8 4.8 copy.48
  453.6 9.6 %copy.49 = f32[2,2,768,768]{2,3,1,0:T(8,128)} copy(f32[2,2,768,768]{3,2,1,0:T(8,128)} %bitcast.89) | data formatting | bytes 18874368 | tf_op jit(solution)/shard_map/reshape | solution.py:63
  463.2 19.5 %collective-permute-done.6 = bf16[2,2,1280,256]{3,2,1,0:T(8,128)(2,1)} collective-permute-done((bf16[2,2,1280,256]{3,2,1,0:T(8,128)(2,1)}, bf16[2,2,1280,256]{3,2,1,0:T(8,128)(2,1)}, u32[]{:S(2)}, u32[]{:S(2)}) %collective-permute-start.6) | collective-permute-done | bytes 2621472 | tf_op jit(solution)/shard_map/ppermute | solution.py:20
  482.7 6.7 %pad_maximum_fusion = bf16[2,2,768,1280]{3,2,1,0:T(8,128)(2,1)} fusion(bf16[2,2,1280,256]{3,2,1,0:T(8,128)(2,1)} %collective-permute-done.7, bf16[2,2,1280,256]{3,2,1,0:T(8,128)(2,1)} %collective-permute-done.6, bf16[2,2,256,768]{3,2,1,0:T(8,128)(2,1)} %copy-done.5, bf16[2,2,768,768]{3,2,1,0:T(8,128)(2,1)} %fusion.1, ...), kind=kLoop, calls=%fused_computation.20 | loop fusion | flops 39321600 | bytes 20971520 | tf_op jit(solution)/shard_map/concatenate | solution.py:24
  489.4 10.7 %copy.41 = bf16[2,2,768,1280]{2,3,1,0:T(8,128)(2,1)} copy(bf16[2,2,768,1280]{3,2,1,0:T(8,128)(2,1)} %pad_maximum_fusion) | data formatting | bytes 15728640 | tf_op jit(solution)/shard_map/slice | solution.py:117
  500.1 7.1 %copy.42 = bf16[2,2,768,5,256]{2,4,1,0,3:T(8,128)(2,1)} copy(bf16[2,2,768,5,256]{2,4,3,1,0:T(8,128)(2,1)} %bitcast.91) | data formatting | bytes 15728640 | tf_op jit(solution)/shard_map/reshape | solution.py:69
  507.2 10.0 %gather_fusion.10 = bf16[9,2,2,768,256]{3,4,2,1,0:T(8,128)(2,1)} fusion(bf16[2,2,768,5,256]{2,4,1,0,3:T(8,128)(2,1)} %copy.42, s32[1024]{0:T(1024)S(1)} %pad_clamp_fusion), kind=kCustom, calls=%fused_computation.11.clone | custom fusion | bytes 28311588 | tf_op jit(solution)/shard_map/jit(_take)/gather | solution.py:71
  517.2 7.1 %broadcast_select_fusion.1 = bf16[9,2,2,768,256]{3,4,2,1,0:T(8,128)(2,1)S(1)} fusion(bf16[9,2,2,768,256]{3,4,2,1,0:T(8,128)(2,1)} %gather_fusion.10, pred[9]{0:T(512)(128)(4,1)S(1)} %compare_and_fusion), kind=kLoop, calls=%fused_computation.13 | loop fusion | flops 7077888 | bytes 28311560 | tf_op jit(solution)/shard_map/jit(_take)/select_n | solution.py:71
  524.2 3.9 convolution_bitcast_fusion.1
  528.1 4.8 copy.45
  532.9 10.2 %fusion = bf16[2,2,768,768]{2,3,1,0:T(8,128)(2,1)} fusion(f32[2,2,768,768]{2,3,1,0:T(8,128)} %copy.49, f32[2,2,768,3,256]{2,4,3,1,0:T(8,128)} %copy.45), kind=kLoop, calls=%fused_computation.17 | loop fusion | flops 4718592 | bytes 23592960 | tf_op jit(solution)/shard_map/convert_element_type | solution.py:125
  543.1 6.6 %copy.50 = bf16[2,2,768,768]{3,2,1,0:T(8,128)(2,1)} copy(bf16[2,2,768,768]{2,3,1,0:T(8,128)(2,1)} %fusion) | data formatting | bytes 9437184 | tf_op jit(solution)/shard_map/convert_element_type | solution.py:125
  (72 shorter events, 7.7 us)
Async XLA Ops:
  6.5 12.7 %copy-start = (s32[48]{0:T(128)S(1)}, s32[48]{0:T(128)}, u32[]{:S(2)}) copy-start(s32[48]{0:T(128)} %param.20) | copy-start | bytes 580
  6.5 9.6 %copy-start.9 = (s32[48,3]{0,1:T(4,128)S(1)}, s32[48,3]{0,1:T(4,128)}, u32[]{:S(2)}) copy-start(s32[48,3]{0,1:T(4,128)} %param.19) | copy-start | bytes 1732
  6.5 11.3 %copy-start.8 = (f32[12288]{0:T(1024)S(1)}, f32[12288]{0:T(1024)}, u32[]{:S(2)}) copy-start(f32[12288]{0:T(1024)} %param.21) | copy-start | bytes 147460
  6.5 223.0 %all-reduce.2.cloned.1.call-start = ((), (), s32[]{:S(2)}) async-start(), calls=%async_computation | async-start | bytes 2359296 | tf_op jit(solution)/shard_map/psum | solution.py:12
  11.5 98.8 %collective-permute-start.1 = (bf16[2,2,256,768]{3,2,1,0:T(8,128)(2,1)}, bf16[2,2,256,768]{3,2,1,0:T(8,128)(2,1)S(1)}, u32[]{:S(2)}, u32[]{:S(2)}) collective-permute-start(bf16[2,2,256,768]{3,2,1,0:T(8,128)(2,1)} %get-tuple-element.21), channel_id=1, source_target_pairs={{16,0},{32,16},{48,32},{64,48},{80,64},{96,80},{112,96},{128,112},... | collective-permute-start | bytes 4718600 | tf_op jit(solution)/shard_map/ppermute | solution.py:23
  14.1 92.0 %collective-permute-start = (bf16[2,2,256,768]{3,2,1,0:T(8,128)(2,1)}, bf16[2,2,256,768]{3,2,1,0:T(8,128)(2,1)}, u32[]{:S(2)}, u32[]{:S(2)}) collective-permute-start(bf16[2,2,256,768]{3,2,1,0:T(8,128)(2,1)} %get-tuple-element.22), channel_id=1, source_target_pairs={{0,16},{16,32},{32,48},{48,64},{64,80},{80,96},{96,112},{112,128},... | collective-permute-start | bytes 4718600 | tf_op jit(solution)/shard_map/ppermute | solution.py:20
  110.5 13.4 %copy-start.3 = (bf16[2,2,1280,768]{3,2,1,0:T(8,128)(2,1)}, bf16[2,2,1280,768]{3,2,1,0:T(8,128)(2,1)S(1)}, u32[]{:S(2)}) copy-start(bf16[2,2,1280,768]{3,2,1,0:T(8,128)(2,1)S(1)} %constant_dynamic-update-slice_fusion) | copy-start | bytes 23592964
  113.4 130.0 %collective-permute-start.2 = (bf16[2,2,1280,256]{3,2,1,0:T(8,128)(2,1)}, bf16[2,2,1280,256]{3,2,1,0:T(8,128)(2,1)}, u32[]{:S(2)}, u32[]{:S(2)}) collective-permute-start(bf16[2,2,1280,256]{3,2,1,0:T(8,128)(2,1)} %get-tuple-element.17), channel_id=1, source_target_pairs={{0,1},{1,2},{2,3},{3,4},{4,5},{5,6},{6,7},{7,8},{8,9},{9,10},{10,1... | collective-permute-start | bytes 7864328 | tf_op jit(solution)/shard_map/ppermute | solution.py:20
  116.8 126.6 %collective-permute-start.3 = (bf16[2,2,1280,256]{3,2,1,0:T(8,128)(2,1)}, bf16[2,2,1280,256]{3,2,1,0:T(8,128)(2,1)}, u32[]{:S(2)}, u32[]{:S(2)}) collective-permute-start(bf16[2,2,1280,256]{3,2,1,0:T(8,128)(2,1)} %get-tuple-element.18), channel_id=1, source_target_pairs={{1,0},{2,1},{3,2},{4,3},{5,4},{6,5},{7,6},{8,7},{9,8},{10,9},{11,1... | collective-permute-start | bytes 7864328 | tf_op jit(solution)/shard_map/ppermute | solution.py:23
  277.8 7.1 %copy-start.6 = (bf16[3,3,256,256]{3,2,1,0:T(8,128)(2,1)S(1)}, bf16[3,3,256,256]{3,2,1,0:T(8,128)(2,1)}, u32[]{:S(2)}) copy-start(bf16[3,3,256,256]{3,2,1,0:T(8,128)(2,1)} %param.18) | copy-start | bytes 3538948
  313.9 100.5 %copy-start.4 = (bf16[2,2,768,768]{3,2,1,0:T(8,128)(2,1)S(1)}, bf16[2,2,768,768]{3,2,1,0:T(8,128)(2,1)}, u32[]{:S(2)}) copy-start(bf16[2,2,768,768]{3,2,1,0:T(8,128)(2,1)} %fusion.1) | copy-start | bytes 14155780
  316.2 97.1 %collective-permute-start.4 = (bf16[2,2,256,768]{3,2,1,0:T(8,128)(2,1)S(1)}, bf16[2,2,256,768]{3,2,1,0:T(8,128)(2,1)S(1)}, u32[]{:S(2)}, u32[]{:S(2)}) collective-permute-start(bf16[2,2,256,768]{3,2,1,0:T(8,128)(2,1)S(1)} %get-tuple-element.19), channel_id=1, source_target_pairs={{0,16},{16,32},{32,48},{48,64},{64,80},{80,96},{96,112},{112,128},... | collective-permute-start | bytes 4718600 | tf_op jit(solution)/shard_map/ppermute | solution.py:20
  318.2 95.1 %collective-permute-start.5 = (bf16[2,2,256,768]{3,2,1,0:T(8,128)(2,1)S(1)}, bf16[2,2,256,768]{3,2,1,0:T(8,128)(2,1)S(1)}, u32[]{:S(2)}, u32[]{:S(2)}) collective-permute-start(bf16[2,2,256,768]{3,2,1,0:T(8,128)(2,1)S(1)} %get-tuple-element.20), channel_id=1, source_target_pairs={{16,0},{32,16},{48,32},{64,48},{80,64},{96,80},{112,96},{128,112},... | collective-permute-start | bytes 4718600 | tf_op jit(solution)/shard_map/ppermute | solution.py:23
  413.3 1.1 copy-start.5
  415.0 3.1 copy-start.2
  420.7 61.9 %collective-permute-start.6 = (bf16[2,2,1280,256]{3,2,1,0:T(8,128)(2,1)}, bf16[2,2,1280,256]{3,2,1,0:T(8,128)(2,1)}, u32[]{:S(2)}, u32[]{:S(2)}) collective-permute-start(bf16[2,2,1280,256]{3,2,1,0:T(8,128)(2,1)} %get-tuple-element.14), channel_id=1, source_target_pairs={{0,1},{1,2},{2,3},{3,4},{4,5},{5,6},{6,7},{7,8},{8,9},{9,10},{10,1... | collective-permute-start | bytes 7864328 | tf_op jit(solution)/shard_map/ppermute | solution.py:20
  422.7 60.0 %collective-permute-start.7 = (bf16[2,2,1280,256]{3,2,1,0:T(8,128)(2,1)}, bf16[2,2,1280,256]{3,2,1,0:T(8,128)(2,1)}, u32[]{:S(2)}, u32[]{:S(2)}) collective-permute-start(bf16[2,2,1280,256]{3,2,1,0:T(8,128)(2,1)} %get-tuple-element.16), channel_id=1, source_target_pairs={{1,0},{2,1},{3,2},{4,3},{5,4},{6,5},{7,6},{8,7},{9,8},{10,9},{11,1... | collective-permute-start | bytes 7864328 | tf_op jit(solution)/shard_map/ppermute | solution.py:23
  517.2 7.1 %copy-start.7 = (bf16[3,3,256,256]{3,2,1,0:T(8,128)(2,1)S(1)}, bf16[3,3,256,256]{3,2,1,0:T(8,128)(2,1)}, u32[]{:S(2)}) copy-start(bf16[3,3,256,256]{3,2,1,0:T(8,128)(2,1)} %param.18) | copy-start | bytes 3538948
  532.9 16.8 %copy-start.1 = (s32[48]{0:T(128)S(1)}, s32[48]{0:T(128)}, u32[]{:S(2)}) copy-start(s32[48]{0:T(128)} %param.20) | copy-start | bytes 580
Sparse Core Ops, SparseCore 0:
  10.0 219.4 all-reduce.1
where the time goes:
time: 558 us; the launch traced here: 557 us
  waiting for transfers between devices  278 us (50%)
  local copies, waits for them, and re-layouts  149 us (27%)
  other arithmetic  67.9 us (12%)
  starting transfers between devices  24.3 us (4%)
  matrix products  22.6 us (4%)
  between operations  13.8 us (2%)
    ppermute x4, waiting for transfers between devices, with_halo(): lax.ppermute(lax.slice_in_dim(block, block.shape[dim] - width, None, axis...  194 us
    psum x1, waiting for transfers between devices, broadcast(): return lax.psum(kept, axis)  84.9 us
    gather x2, local copies, waits for them, and re-layouts, left_apply(): jnp.take(pieces, relative, axis=2)  20 us
    gather x2, local copies, waits for them, and re-layouts, right_apply(): jnp.take(pieces, relative, axis=3)  20 us
    select_n x3, other arithmetic, left_apply(): jnp.take(pieces, relative, axis=2)  17.7 us
    ppermute x4, starting transfers between devices, with_halo(): lax.ppermute(lax.slice_in_dim(block, 0, width, axis=dim), axis, backward)  15 us
    dot_general x2, matrix products, left_apply(): jnp.einsum('ikab,rpikbc->rpiac', matrix, picked, preferred_element_type=j...  14.3 us
    reshape x2, local copies, waits for them, and re-layouts, right_apply(): source_operator.reshape(copies, halves, source_rows, breadth // block_siz...  14.1 us
  transfers between devices with their start and end apart: 9, of which 4 were waited for; matrix products, arithmetic and copies ran while one was open for 16% of the time, Pallas kernels for 0%

commit v1 on v0

v1 whole, which is shorter than its diff:
```python
import functools

import jax
import jax.numpy as jnp
from jax import lax
from jax.experimental import pallas as pl
from jax.experimental.pallas import tpu as pltpu
from jax.sharding import PartitionSpec as P

MESH = pl.DeviceIdType.MESH
BF = jnp.bfloat16
F32 = jnp.float32
CHAIN = 6
SWAP, CHAIN_R, CHAIN_L = 0, CHAIN, 2 * CHAIN
IN = CHAIN_L + CHAIN
DHALO = IN + 6
CHALO = DHALO + 12
OUT = CHALO + 8
COPIES = OUT + 6
ORDER = (0, 2, 1)


def kernel(nk, nb, density, panel, e_sub, e_lane, out, dext, cext, res, orow, ocol, wrow, wcol, ssem, rsem, lsem):
    bs = panel.shape[1]
    tile = density.shape[1]
    nr = tile // bs
    k, b = lax.axis_index("ket"), lax.axis_index("bra")
    core, hi, lo, z, nz = k % 2, (k // 2) % 2, b % 2, b // 2, nb // 2
    flip = b + 1 - 2 * lo
    colour = (hi + lo) % 2
    keep, give = 2 * colour, 2 - 2 * colour
    pair = (k, flip)
    swap = (k + 2 - 4 * hi, flip)
    up = ((k + nk - 1) % nk, core * b + (1 - core) * flip)
    down = ((k + 1) % nk, (1 - core) * b + core * flip)
    left, right = (k, (b + nb - 2) % nb), (k, (b + 2) % nb)
    dist = (z + nz - (k // 2) % nz) % nz

    def cols(half):
        return pl.ds(pl.multiple_of(bs + half * tile, bs), tile)

    mine, other = cols(lo), cols(1 - lo)
    first, last = pl.ds(bs, bs), pl.ds(nr * bs, bs)
    inner = pl.ds(bs, tile)
    above, below = pl.ds(0, bs), pl.ds((nr + 1) * bs, bs)
    lcol, rcol = pl.ds(bs, bs), pl.ds(2 * nr * bs, bs)
    lhalo, rhalo = pl.ds(0, bs), pl.ds((2 * nr + 1) * bs, bs)

    def remote(index, src, dst, device):
        return pltpu.make_async_remote_copy(
            src_ref=src, dst_ref=dst, send_sem=ssem.at[index], recv_sem=rsem.at[index],
            device_id=device, device_id_type=MESH,
        )

    own_tiles = [
        pltpu.make_async_copy(density.at[keep + m], dext.at[m, inner, mine], lsem.at[m]) for m in range(2)
    ]
    own_cols = pltpu.make_async_copy(panel, ocol.at[pl.ds(nr * lo, nr)], lsem.at[2])
    own_rows = pltpu.make_async_copy(ocol.at[pl.ds(nr * core, nr)], orow, lsem.at[3])
    for copy in own_tiles:
        copy.start()
    own_cols.start()

    barrier = pltpu.get_barrier_semaphore()
    for device in (pair, swap, up, down, left, right):
        pl.semaphore_signal(barrier, inc=1, device_id=device, device_id_type=MESH)
    pl.semaphore_wait(barrier, 6)

    part = nr * bs // CHAIN

    def piece(j):
        return j * part // bs, pl.ds(j * part % bs, part)

    swaps = []
    for j in range(CHAIN):
        row, where = piece(j)
        swaps.append(remote(SWAP + j, panel.at[row, where], ocol.at[nr * lo + row, where], swap))
        swaps[j].start()
    source = dist == 0
    swapped_source = source & (core != lo)

    def rows(r):
        return pl.ds(r * bs, bs)

    give_tiles = [
        [
            remote(IN + 3 * m + r, density.at[give + m, rows(r)], dext.at[m, rows(r + 1), mine], pair)
            for r in range(3)
        ]
        for m in range(2)
    ]

    halo = []
    for m in range(2):
        at = DHALO + 6 * m
        halo.append(
            [
                remote(at, density.at[keep + m, rows(0)], dext.at[m, below, mine], up),
                remote(at + 1, density.at[keep + m, rows(nr - 1)], dext.at[m, above, mine], down),
                remote(at + 2, dext.at[m, first, other], dext.at[m, below, other], up),
                remote(at + 3, dext.at[m, last, other], dext.at[m, above, other], down),
                remote(at + 4, dext.at[m, inner, lcol], dext.at[m, inner, rhalo], left),
                remote(at + 5, dext.at[m, inner, rcol], dext.at[m, inner, lhalo], right),
            ]
        )
    chalo = []
    for m in range(2):
        at = CHALO + 4 * m
        chalo.append(
            [
                remote(at, cext.at[m, first, pl.ds(bs, 2 * tile)], cext.at[m, below, pl.ds(bs, 2 * tile)], up),
                remote(at + 1, cext.at[m, last, pl.ds(bs, 2 * tile)], cext.at[m, above, pl.ds(bs, 2 * tile)], down),
                remote(at + 2, cext.at[m, inner, lcol], cext.at[m, inner, rhalo], left),
                remote(at + 3, cext.at[m, inner, rcol], cext.at[m, inner, lhalo], right),
            ]
        )

    def chain(j, act):
        row, where = piece(j)
        target = orow.at[row, where]

        def send(from_ref, index, device):
            return pltpu.make_async_remote_copy(
                src_ref=from_ref, dst_ref=target, send_sem=ssem.at[index + j], recv_sem=rsem.at[CHAIN_R + j],
                device_id=device, device_id_type=MESH,
            )

        on_right, on_left = send(target, CHAIN_R, right), send(target, CHAIN_L, left)
        held = ocol.at[nr * core + row, where]
        to_right = (dist != 0) & (dist < nz // 2)
        to_left = dist > nz // 2 + 1
        if act == "forward":

            @pl.when(swapped_source)
            def _():
                swaps[j].wait_recv()

            @pl.when(source)
            def _():
                send(held, CHAIN_R, right).start()
                send(held, CHAIN_L, left).start()

            @pl.when(dist != 0)
            def _():
                on_right.wait_recv()

            @pl.when(to_right)
            def _():
                on_right.start()

            @pl.when(to_left)
            def _():
                on_left.start()

        else:

            @pl.when(source | to_right)
            def _():
                on_right.wait_send()

            @pl.when(source | to_left)
            def _():
                on_left.wait_send()

    own_cols.wait()
    for r in ORDER:
        give_tiles[0][r].start()
    halo[0][0].start()
    halo[0][1].start()
    chain(0, "forward")
    chain(1, "forward")
    give_tiles[0][0].wait_recv()
    halo[0][2].start()
    chain(2, "forward")
    chain(3, "forward")
    give_tiles[0][2].wait_recv()
    halo[0][3].start()
    chain(4, "forward")
    chain(5, "forward")
    own_tiles[0].wait()
    give_tiles[0][1].wait_recv()
    halo[0][4].start()
    halo[0][5].start()
    for r in ORDER:
        give_tiles[0][r].wait_send()
    for r in ORDER:
        give_tiles[1][r].start()
    halo[1][0].start()
    halo[1][1].start()

    step = 32

    def weigh(source, target, index, at):
        def chunk(c, carry):
            where = pl.ds(pl.multiple_of(c * step, step), step)
            x = e_sub[at, where] - e_lane[at]
            u = jnp.exp(jnp.abs(x) * -0.25)
            q = u * u
            q = q * q
            spectral = jnp.where(x >= 0, 1.0, q) / (1.0 + q) * u
            target[index, where] = (source[index, where].astype(F32) * spectral).astype(BF)
            return carry

        lax.fori_loop(0, bs // step, chunk, 0)

    def weigh_all(source, target, count, offset):
        def one(p, carry):
            weigh(source, target, p, p + offset)
            return carry

        lax.fori_loop(0, count, one, 0)

    for j in range(CHAIN):

        @pl.when(jnp.logical_not(swapped_source))
        def _():
            swaps[j].wait_recv()

    @pl.when(source)
    def _():
        own_rows.start()
        own_rows.wait()

    weigh_all(orow, wrow, nr, 0)
    weigh_all(ocol, wcol, 2 * nr, nr)

    def block_row(m, i, source, row_op, col_op, sign, store):
        def half(h, carry):
            base = pl.multiple_of(h * tile, tile)
            through_rows = jnp.dot(
                row_op[i], source[m, pl.ds(i * bs, 3 * bs), pl.ds(pl.multiple_of(base + bs, bs), tile)],
                preferred_element_type=F32,
            )
            for j in range(nr):
                at = pl.multiple_of(base + j * bs, bs)
                through_cols = lax.dot_general(
                    source[m, rows(i + 1), pl.ds(at, 3 * bs)], col_op[h * nr + j],
                    (((1,), (1,)), ((), ())), preferred_element_type=F32,
                )
                store(m, i, at, (sign * (through_rows[:, j * bs : (j + 1) * bs] - through_cols)).astype(BF))
            return carry

        lax.fori_loop(0, 2, half, 0)

    def store_c(m, i, at, value):
        cext[m, rows(i + 1), pl.ds(pl.multiple_of(at + bs, bs), bs)] = value

    def store_out(m, i, at, value):
        res[m, rows(i), pl.ds(at, bs)] = value

    def commutand(m):
        for copy in halo[m]:
            copy.wait_recv()
        for i in ORDER:
            block_row(m, i, dext, wrow, wcol, 1.0, store_c)
            if i == 0:
                chalo[m][0].start()
            if i == nr - 1:
                chalo[m][1].start()
        chalo[m][2].start()
        chalo[m][3].start()

    def res_cols(half):
        return pl.ds(pl.multiple_of(half * tile, tile), tile)

    back = [
        [
            remote(OUT + 3 * m + i, res.at[m, rows(i), res_cols(1 - lo)], out.at[keep + m, rows(i)], pair)
            for i in range(3)
        ]
        for m in range(2)
    ]
    keep_out = [
        [
            pltpu.make_async_copy(res.at[m, rows(i), res_cols(lo)], out.at[keep + m, rows(i)], lsem.at[4 + 3 * m + i])
            for i in range(3)
        ]
        for m in range(2)
    ]

    def dissipated(m):
        for copy in chalo[m]:
            copy.wait_recv()
        for i in (1, 0, 2):
            block_row(m, i, cext, orow, ocol, -1.0, store_out)
            back[m][i].start()
            keep_out[m][i].start()

    commutand(0)
    own_tiles[1].wait()
    for r, at in ((0, (2,)), (2, (3,)), (1, (4, 5))):
        give_tiles[1][r].wait_recv()
        for a in at:
            halo[1][a].start()
    dissipated(0)
    commutand(1)
    dissipated(1)

    for j in range(CHAIN):
        swaps[j].wait_send()
        chain(j, "end")
    for r in range(3):
        give_tiles[1][r].wait_send()
    for m in range(2):
        for copy in halo[m] + chalo[m]:
            copy.wait_send()
        for i in range(3):
            keep_out[m][i].wait()
            back[m][i].wait_send()
            back[m][i].wait_recv()


def body(density, coupling, block_cols, block_count, energies):
    copies, halves, tile, _ = density.shape
    nr, slots, bs, _ = coupling.shape
    nk, nb = lax.axis_size("ket"), lax.axis_size("bra")
    k, b = lax.axis_index("ket"), lax.axis_index("bra")
    total = block_cols.shape[0]

    start = b * nr
    columns = lax.dynamic_slice_in_dim(block_cols, start, nr, 0)
    counts = lax.dynamic_slice_in_dim(block_count, start, nr, 0)
    used = jnp.arange(slots, dtype=jnp.int32)[None, :] < counts[:, None]
    place = columns - (start + jnp.arange(nr, dtype=jnp.int32))[:, None]
    zero = jnp.zeros((nr, bs, bs), coupling.dtype)
    blocks = []
    for offset in (-1, 0, 1):
        block = zero
        for s in range(slots):
            holds = (used[:, s] & (place[:, s] == offset))[:, None, None]
            block = jnp.where(holds, coupling[:, s], block)
        blocks.append(block)
    panel = jnp.concatenate(blocks, axis=2)

    levels = energies.reshape(total, bs)
    levels = jnp.concatenate([levels[:1], levels, levels[-1:]], axis=0)

    def level_sets(at, count):
        here = lax.dynamic_slice_in_dim(levels, at, count + 2, 0)
        return here[1 : count + 1], jnp.concatenate([here[:count], here[1 : count + 1], here[2:]], axis=1)

    row_sub, row_lane = level_sets(k * nr, nr)
    col_sub, col_lane = level_sets(b // 2 * 2 * nr, 2 * nr)
    e_sub = jnp.concatenate([row_sub, col_sub], axis=0)[:, :, None]
    e_lane = jnp.concatenate([row_lane, col_lane], axis=0)[:, None, :]

    any_space = pl.BlockSpec(memory_space=pl.ANY)
    vmem = pl.BlockSpec(memory_space=pltpu.VMEM)
    out = pl.pallas_call(
        functools.partial(kernel, nk, nb),
        out_shape=jax.ShapeDtypeStruct((copies * halves, tile, tile), density.dtype),
        in_specs=[any_space, any_space, vmem, vmem],
        out_specs=any_space,
        scratch_shapes=[
            pltpu.VMEM((2, tile + 2 * bs, 2 * tile + 2 * bs), BF),
            pltpu.VMEM((2, tile + 2 * bs, 2 * tile + 2 * bs), BF),
            pltpu.VMEM((2, tile, 2 * tile), BF),
            pltpu.VMEM((nr, bs, 3 * bs), BF),
            pltpu.VMEM((2 * nr, bs, 3 * bs), BF),
            pltpu.VMEM((nr, bs, 3 * bs), BF),
            pltpu.VMEM((2 * nr, bs, 3 * bs), BF),
            pltpu.SemaphoreType.DMA((COPIES,)),
            pltpu.SemaphoreType.DMA((COPIES,)),
            pltpu.SemaphoreType.DMA((10,)),
        ],
        compiler_params=pltpu.CompilerParams(
            collective_id=0, has_side_effects=True, vmem_limit_bytes=58 << 20
        ),
        name="dissipator",
    )(density.reshape(copies * halves, tile, tile), panel, e_sub, e_lane)
    return out.reshape(density.shape)


def solution(mesh):
    return jax.shard_map(
        body,
        mesh=mesh,
        in_specs=(P(None, None, "ket", "bra"), P("bra", None, None, None), P(), P(), P()),
        out_specs=P(None, None, "ket", "bra"),
        check_vma=False,
    )
```

time: 558 us -> 154 us (0.28)
  the two profiles are of different devices: /device:TPU:92 before, /device:TPU:45 now
where the time goes in v1:
time: 154 us
  Pallas kernels  143 us (93%)
  local copies, waits for them, and re-layouts  9.31 us (6%)
  other arithmetic  2.1 us (1%)
    pallas_call x1, Pallas kernels, body(): pl.pallas_call(functools.partial(kernel, nk, nb), out_shape=jax.ShapeDtyp...  143 us
    unnamed x3, local copies, waits for them, and re-layouts  4.83 us

profile of v1, /device:TPU:45, one launch (start us, length us, event | category | flops | bytes accessed | tf_op | source)
XLA Modules:
  0.0 154.1 jit_solution(13837812361219335681)
XLA Ops:
  0.0 0.0 copy-start
  0.0 0.8 dynamic_slice.12
  0.8 0.8 dynamic-slice_subtract_fusion
  1.6 0.7 fusion.6
  2.3 0.8 reshape.134
  3.3 0.6 broadcast_in_dim.80.e_lane
  3.9 1.5 copy.9.e_sub
  5.3 0.0 copy-done
  5.3 0.2 fusion.1
  5.6 1.1 pad_maximum_fusion.panel
  6.6 142.6 %dissipator.1 = bf16[4,768,768]{2,1,0:T(8,128)(2,1)} custom-call(bf16[4,768,768]{2,1,0:T(8,128)(2,1)} %bitcast.55, bf16[3,256,768]{2,1,0:T(8,128)(2,1)} %pad_maximum_fusion.panel, f32[9,256,1]{2,1,0:T(8,128)} %copy.9.e_sub, f32[9,1,768]{2,1,0:T(1,128)} %broadcast_in_dim.80.e_lane), custom_call_target="tpu_custom_call" | custom-call | tf_op jit(solution)/shard_map/dissipator/pallas_call | solution.py:349
  149.3 4.8 %copy.14 = bf16[2,2,768,768]{3,2,1,0:T(8,128)(2,1)} copy(bf16[2,2,768,768]{3,2,1,0:T(8,128)(2,1)} %bitcast.54) | data formatting | bytes 9437184
  (8 shorter events, 0.1 us)
Async XLA Ops:
  0.0 5.3 %copy-start = (bf16[3,3,256,256]{3,2,1,0:T(8,128)(2,1)S(1)}, bf16[3,3,256,256]{3,2,1,0:T(8,128)(2,1)}, u32[]{:S(2)}) copy-start(bf16[3,3,256,256]{3,2,1,0:T(8,128)(2,1)} %param.6) | copy-start | bytes 3538948

commit v2 on v1

v2 whole, which is shorter than its diff:
```python
import functools

import jax
import jax.numpy as jnp
from jax import lax
from jax.experimental import pallas as pl
from jax.experimental.pallas import tpu as pltpu
from jax.sharding import PartitionSpec as P

MESH = pl.DeviceIdType.MESH
BF = jnp.bfloat16
F32 = jnp.float32
CHAIN = 6
SWAP = 0
RELAY = SWAP + CHAIN
RING = RELAY + CHAIN
IN = RING + CHAIN
DHALO = IN + 6
CHALO = DHALO + 12
OUT = CHALO + 8
COPIES = OUT + 6
ORDER = (0, 2, 1)
STEP = 32


def kernel(
    nk, nb, density, coupling, levels, block_cols, block_count, out,
    dext, cext, res, rraw, craw, orow, ocol, wrow, wcol, ssem, rsem, lsem,
):
    nr, slots, bs, _ = coupling.shape
    tile = nr * bs
    total = block_cols.shape[0]
    k, b = lax.axis_index("ket"), lax.axis_index("bra")
    core, hi, lo, z, nz = k % 2, (k // 2) % 2, b % 2, b // 2, nb // 2
    flip = b + 1 - 2 * lo
    colour = (hi + lo) % 2
    keep, give = 2 * colour, 2 - 2 * colour
    pair = (k, flip)
    swap = (k + 2 - 4 * hi, flip)
    sibling = (k + 1 - 2 * core, b)
    up = ((k + nk - 1) % nk, core * b + (1 - core) * flip)
    down = ((k + 1) % nk, (1 - core) * b + core * flip)
    left, right = (k, (b + nb - 2) % nb), (k, (b + 2) % nb)
    after = (k, (b + 2 + core * (nb - 4)) % nb)
    away = (z + nz - (k // 2) % nz) % nz
    dist = (away + core * (2 * nz - 2 * away)) % nz
    source = dist == 0
    swapped_source = source & (core != lo)

    def cols(half):
        return pl.ds(pl.multiple_of(bs + half * tile, bs), tile)

    def rows(r):
        return pl.ds(r * bs, bs)

    mine, other = cols(lo), cols(1 - lo)
    first, last = pl.ds(bs, bs), pl.ds(nr * bs, bs)
    inner, across = pl.ds(bs, tile), pl.ds(bs, 2 * tile)
    above, below = pl.ds(0, bs), pl.ds((nr + 1) * bs, bs)
    lcol, rcol = pl.ds(bs, bs), pl.ds(2 * nr * bs, bs)
    lhalo, rhalo = pl.ds(0, bs), pl.ds((2 * nr + 1) * bs, bs)

    def remote(sends, receives, src, dst, device):
        return pltpu.make_async_remote_copy(
            src_ref=src, dst_ref=dst, send_sem=ssem.at[sends], recv_sem=rsem.at[receives],
            device_id=device, device_id_type=MESH,
        )

    own_tiles = [
        pltpu.make_async_copy(density.at[keep + m], dext.at[m, inner, mine], lsem.at[m]) for m in range(2)
    ]
    own_cols = pltpu.make_async_copy(coupling, craw.at[pl.ds(nr * lo, nr)], lsem.at[2])
    own_rows = pltpu.make_async_copy(craw.at[pl.ds(nr * core, nr)], rraw, lsem.at[3])
    own_cols.start()
    for copy in own_tiles:
        copy.start()

    barrier = pltpu.get_barrier_semaphore()
    for device in (pair, swap, up, down, left, right):
        pl.semaphore_signal(barrier, inc=1, device_id=device, device_id_type=MESH)
    pl.semaphore_wait(barrier, 6)

    parts = CHAIN // nr
    part = bs // parts

    def piece(ref, base, j):
        return ref.at[base + j // parts, :, pl.ds(pl.multiple_of(j % parts * part, part), part)]

    def swap_copy(j):
        return remote(SWAP + j, SWAP + j, piece(coupling, 0, j), piece(craw, nr * lo, j), swap)

    def relay_copy(j):
        got = piece(craw, nr * (1 - lo), j)
        return remote(RELAY + j, SWAP + j, got, got, sibling)

    def ring_copy(j, start):
        target = piece(rraw, 0, j)
        return remote(RING + j, RING + j, piece(craw, nr * core, j) if start else target, target, after)

    give_tiles = [
        [
            remote(IN + 3 * m + r, IN + 3 * m + r, density.at[give + m, rows(r)], dext.at[m, rows(r + 1), mine], pair)
            for r in range(3)
        ]
        for m in range(2)
    ]

    halo, chalo = [], []
    for m in range(2):
        moves = (
            (density.at[keep + m, rows(0)], dext.at[m, below, mine], up),
            (density.at[keep + m, rows(nr - 1)], dext.at[m, above, mine], down),
            (dext.at[m, first, other], dext.at[m, below, other], up),
            (dext.at[m, last, other], dext.at[m, above, other], down),
            (dext.at[m, inner, lcol], dext.at[m, inner, rhalo], left),
            (dext.at[m, inner, rcol], dext.at[m, inner, lhalo], right),
        )
        halo.append([remote(DHALO + 6 * m + n, DHALO + 6 * m + n, *move) for n, move in enumerate(moves)])
        moves = (
            (cext.at[m, first, across], cext.at[m, below, across], up),
            (cext.at[m, last, across], cext.at[m, above, across], down),
            (cext.at[m, inner, lcol], cext.at[m, inner, rhalo], left),
            (cext.at[m, inner, rcol], cext.at[m, inner, lhalo], right),
        )
        chalo.append([remote(CHALO + 4 * m + n, CHALO + 4 * m + n, *move) for n, move in enumerate(moves)])

    def order_panel(raw, p, g, operator, weighted):
        coefs = [
            [
                ((block_cols[g, s] == g + o) & (s < block_count[g])).astype(jnp.int32).astype(F32)
                for s in range(slots)
            ]
            for o in (-1, 0, 1)
        ]
        here = jnp.transpose(jnp.broadcast_to(levels[pl.ds(g, 1), :], (128, bs)))
        for c in range(bs // STEP):
            at = pl.ds(c * STEP, STEP)
            held = [raw[p, s, at].astype(F32) for s in range(slots)]
            mine_levels = jnp.concatenate([here[c * STEP : (c + 1) * STEP]] * (bs // 128), axis=1)
            for n in range(3):
                there = levels[pl.ds((g + total + n - 1) % total, 1), :]
                x = mine_levels - there
                u = jnp.exp(jnp.abs(x) * -0.25)
                q = u * u
                q = q * q
                spectral = jnp.where(x >= 0, 1.0, q) / (1.0 + q) * u
                block = held[0] * coefs[n][0]
                for s in range(1, slots):
                    block = block + held[s] * coefs[n][s]
                operator[p, at, pl.ds(n * bs, bs)] = block.astype(BF)
                weighted[p, at, pl.ds(n * bs, bs)] = (block * spectral).astype(BF)

    col_start = b // 2 * 2 * nr

    def order_col(p):
        order_panel(craw, p, col_start + p, ocol, wcol)

    def service(s):
        j = s - dist
        active = (j >= 0) & (j < CHAIN)

        @pl.when((s < CHAIN) & (s % 2 == core))
        def _():
            swap_copy(s).wait_recv()
            relay_copy(s).start()

        @pl.when(swapped_source & (s < CHAIN) & (s % 2 != core))
        def _():
            swap_copy(s).wait_recv()

        @pl.when(active & source)
        def _():
            ring_copy(j, True).start()

        @pl.when(active & (dist != 0))
        def _():
            ring_copy(j, False).wait_recv()

        @pl.when(active & (dist != 0) & (dist < nz - 1))
        def _():
            ring_copy(j, False).start()

    def serve(begin, end, beside=None):
        def slot(s, carry):
            service(s)
            if beside is not None:
                beside(s - begin)
            return carry

        lax.fori_loop(begin, end, slot, 0)

    def taken(r, next_halo):
        give_tiles[0][r].wait_send()
        give_tiles[1][r].start()
        give_tiles[0][r].wait_recv()
        for n in next_halo:
            halo[0][n].start()

    for i in range(CHAIN // 2):
        swap_copy(2 * i + core).start()
    for r in ORDER:
        give_tiles[0][r].start()
    halo[0][0].start()
    halo[0][1].start()
    own_cols.wait()
    serve(0, 3)
    taken(0, (2,))
    serve(3, 6)
    taken(2, (3,))
    serve(6, 9, lambda p: order_col(nr * lo + p))
    own_tiles[0].wait()
    taken(1, (4, 5))
    halo[1][0].start()
    halo[1][1].start()
    for i in range(CHAIN // 2):

        @pl.when(jnp.logical_not(swapped_source))
        def _():
            swap_copy(2 * i + 1 - core).wait_recv()

    serve(9, 12, lambda p: order_col(nr * (1 - lo) + p))
    serve(12, max(13, CHAIN + nz - 1))

    @pl.when(source)
    def _():
        own_rows.start()
        own_rows.wait()

    def block_half(m, i, h, source_ref, row_op, col_op, store):
        base = pl.multiple_of(h * tile, tile)
        through_rows = jnp.dot(
            row_op[i], source_ref[m, pl.ds(i * bs, 3 * bs), pl.ds(pl.multiple_of(base + bs, bs), tile)],
            preferred_element_type=F32,
        )
        for j in range(nr):
            at = pl.multiple_of(base + j * bs, bs)
            through_cols = lax.dot_general(
                source_ref[m, rows(i + 1), pl.ds(at, 3 * bs)], col_op[h * nr + j],
                (((1,), (1,)), ((), ())), preferred_element_type=F32,
            )
            store(j, through_rows[:, j * bs : (j + 1) * bs], through_cols)

    def commutand_row(m, i):
        def half(h, carry):
            def store(j, through_rows, through_cols):
                at = pl.multiple_of(h * tile + (j + 1) * bs, bs)
                cext[m, rows(i + 1), pl.ds(at, bs)] = (through_rows - through_cols).astype(BF)

            block_half(m, i, h, dext, wrow, wcol, store)
            return carry

        lax.fori_loop(0, 2, half, 0)

    back = [
        [
            remote(OUT + 3 * m + i, OUT + 3 * m + i, res.at[m, rows(i)], out.at[keep + m, rows(i)], pair)
            for i in range(3)
        ]
        for m in range(2)
    ]

    def dissipated_row(m, i):
        def store_other(j, through_rows, through_cols):
            res[m, rows(i), rows(j)] = (through_cols - through_rows).astype(BF)

        def store_mine(j, through_rows, through_cols):
            out[keep + m, rows(i), rows(j)] = (through_cols - through_rows).astype(BF)

        block_half(m, i, 1 - lo, cext, orow, ocol, store_other)
        back[m][i].start()
        block_half(m, i, lo, cext, orow, ocol, store_mine)

    def commutand(m):
        for copy in halo[m]:
            copy.wait_recv()
        for n, i in enumerate(ORDER):
            if m == 0:
                order_panel(rraw, i, k * nr + i, orow, wrow)
            commutand_row(m, i)
            if n < 2:
                chalo[m][n].start()
        chalo[m][2].start()
        chalo[m][3].start()

    def dissipated(m):
        chalo[m][2].wait_recv()
        chalo[m][3].wait_recv()
        dissipated_row(m, 1)
        chalo[m][1].wait_recv()
        dissipated_row(m, 0)
        chalo[m][0].wait_recv()
        dissipated_row(m, 2)

    commutand(0)
    own_tiles[1].wait()
    for r, which in ((0, (2,)), (2, (3,)), (1, (4, 5))):
        give_tiles[1][r].wait_recv()
        for n in which:
            halo[1][n].start()
    dissipated(0)
    commutand(1)
    dissipated(1)

    for i in range(CHAIN // 2):
        swap_copy(2 * i + core).wait_send()
        relay_copy(2 * i + core).wait_send()
    for j in range(CHAIN):

        @pl.when(dist < nz - 1)
        def _():
            ring_copy(j, False).wait_send()

    for r in range(3):
        give_tiles[1][r].wait_send()
    for m in range(2):
        for copy in halo[m] + chalo[m]:
            copy.wait_send()
        for i in range(3):
            back[m][i].wait_send()
            back[m][i].wait_recv()


def body(density, coupling, block_cols, block_count, energies):
    copies, halves, tile, _ = density.shape
    nr, slots, bs, _ = coupling.shape
    nk, nb = lax.axis_size("ket"), lax.axis_size("bra")
    total = block_cols.shape[0]
    any_space = pl.BlockSpec(memory_space=pl.ANY)
    vmem = pl.BlockSpec(memory_space=pltpu.VMEM)
    smem = pl.BlockSpec(memory_space=pltpu.SMEM)
    out = pl.pallas_call(
        functools.partial(kernel, nk, nb),
        out_shape=pltpu.VMEM((copies * halves, tile, tile), density.dtype),
        in_specs=[any_space, any_space, vmem, smem, smem],
        out_specs=vmem,
        scratch_shapes=[
            pltpu.VMEM((2, tile + 2 * bs, 2 * tile + 2 * bs), BF),
            pltpu.VMEM((2, tile + 2 * bs, 2 * tile + 2 * bs), BF),
            pltpu.VMEM((2, tile, tile), BF),
            pltpu.VMEM((nr, slots, bs, bs), BF),
            pltpu.VMEM((2 * nr, slots, bs, bs), BF),
            pltpu.VMEM((nr, bs, 3 * bs), BF),
            pltpu.VMEM((2 * nr, bs, 3 * bs), BF),
            pltpu.VMEM((nr, bs, 3 * bs), BF),
            pltpu.VMEM((2 * nr, bs, 3 * bs), BF),
            pltpu.SemaphoreType.DMA((COPIES,)),
            pltpu.SemaphoreType.DMA((COPIES,)),
            pltpu.SemaphoreType.DMA((4,)),
        ],
        compiler_params=pltpu.CompilerParams(
            collective_id=0, has_side_effects=True, vmem_limit_bytes=52 << 20
        ),
        name="dissipator",
    )(density.reshape(copies * halves, tile, tile), coupling, energies.reshape(total, bs), block_cols, block_count)
    return out.reshape(density.shape)


def solution(mesh):
    return jax.shard_map(
        body,
        mesh=mesh,
        in_specs=(P(None, None, "ket", "bra"), P("bra", None, None, None), P(), P(), P()),
        out_specs=P(None, None, "ket", "bra"),
        check_vma=False,
    )
```

time: 154 us -> 149 us (0.968)
  the two profiles are of different devices: /device:TPU:45 before, /device:TPU:16 now
where the time goes in v2:
time: 149 us; the launch traced here: 148 us
  Pallas kernels  143 us (96%)
  local copies, waits for them, and re-layouts  4.98 us (3%)
    pallas_call x1, Pallas kernels, body(): pl.pallas_call(functools.partial(kernel, nk, nb), out_shape=pltpu.VMEM((c...  143 us
    unnamed x2, local copies, waits for them, and re-layouts  3.55 us

profile of v2, /device:TPU:16, one launch (start us, length us, event | category | flops | bytes accessed | tf_op | source)
XLA Modules:
  0.0 147.8 jit_solution(15121620325516523983)
XLA Ops:
  0.0 1.4 copy.6.block_cols
  1.4 1.4 reshape.10.levels
  2.8 142.8 %dissipator.1 = bf16[4,768,768]{2,1,0:T(8,128)(2,1)S(1)} custom-call(bf16[4,768,768]{2,1,0:T(8,128)(2,1)} %bitcast.3, bf16[3,3,256,256]{3,2,1,0:T(8,128)(2,1)} %coupling.1, f32[48,256]{1,0:T(8,128)} %reshape.10.levels, s32[48,3]{1,0:T(8,128)} %copy.6.block_cols, s32[48]{0:T(128)} %block_count.1), custom_call_target="tpu_custom_call" | custom-call | tf_op jit(solution)/shard_map/dissipator/pallas_call | solution.py:331
  145.6 2.2 %copy.8 = bf16[2,2,768,768]{3,2,1,0:T(8,128)(2,1)} copy(bf16[2,2,768,768]{3,2,1,0:T(8,128)(2,1)S(1)} %bitcast.2) | data formatting | bytes 9437184

commit v3 on v2

v3 whole, which is shorter than its diff:
```python
import functools

import jax
import jax.numpy as jnp
from jax import lax
from jax.experimental import pallas as pl
from jax.experimental.pallas import tpu as pltpu
from jax.sharding import PartitionSpec as P

MESH = pl.DeviceIdType.MESH
BF = jnp.bfloat16
F32 = jnp.float32
CHAIN = 24
SWAP = 0
RELAY = SWAP + CHAIN
RING = RELAY + CHAIN
IN = RING + CHAIN
DHALO = IN + 6
CHALO = DHALO + 12
OUT = CHALO + 8
COPIES = OUT + 12
ORDER = (0, 2, 1)


def kernel(
    nk, nb, density, coupling, levels, block_cols, block_count, out,
    dext, cext, res, rraw, craw, orow, ocol, wrow, wcol, own_levels, ssem, rsem, lsem,
):
    nr, slots, bs, _ = coupling.shape
    tile = nr * bs
    total = block_cols.shape[0]
    k, b = lax.axis_index("ket"), lax.axis_index("bra")
    core, hi, lo, z, nz = k % 2, (k // 2) % 2, b % 2, b // 2, nb // 2
    flip = b + 1 - 2 * lo
    colour = (hi + lo) % 2
    keep, give = 2 * colour, 2 - 2 * colour
    pair = (k, flip)
    swap = (k + 2 - 4 * hi, flip)
    sibling = (k + 1 - 2 * core, b)
    up = ((k + nk - 1) % nk, core * b + (1 - core) * flip)
    down = ((k + 1) % nk, (1 - core) * b + core * flip)
    left, right = (k, (b + nb - 2) % nb), (k, (b + 2) % nb)
    after = (k, (b + 2 + core * (nb - 4)) % nb)
    away = (z + nz - (k // 2) % nz) % nz
    dist = (away + core * (2 * nz - 2 * away)) % nz
    source = dist == 0

    def cols(half):
        return pl.ds(pl.multiple_of(bs + half * tile, bs), tile)

    def rows(r):
        return pl.ds(r * bs, bs)

    mine, other = cols(lo), cols(1 - lo)
    first, last = pl.ds(bs, bs), pl.ds(nr * bs, bs)
    inner, across = pl.ds(bs, tile), pl.ds(bs, 2 * tile)
    above, below = pl.ds(0, bs), pl.ds((nr + 1) * bs, bs)
    lcol, rcol = pl.ds(bs, bs), pl.ds(2 * nr * bs, bs)
    lhalo, rhalo = pl.ds(0, bs), pl.ds((2 * nr + 1) * bs, bs)

    def remote(sends, receives, src, dst, device):
        return pltpu.make_async_remote_copy(
            src_ref=src, dst_ref=dst, send_sem=ssem.at[sends], recv_sem=rsem.at[receives],
            device_id=device, device_id_type=MESH,
        )

    own_tiles = [
        pltpu.make_async_copy(density.at[keep + m], dext.at[m, inner, mine], lsem.at[m]) for m in range(2)
    ]
    own_cols = pltpu.make_async_copy(coupling, craw.at[pl.ds(nr * lo, nr)], lsem.at[2])
    own_rows = pltpu.make_async_copy(craw.at[pl.ds(nr * core, nr)], rraw, lsem.at[3])
    own_cols.start()
    for copy in own_tiles:
        copy.start()

    barrier = pltpu.get_barrier_semaphore()
    for device in (pair, swap, up, down, left, right):
        pl.semaphore_signal(barrier, inc=1, device_id=device, device_id_type=MESH)

    col_start = b // 2 * 2 * nr
    for p in range(3 * nr):
        g = k * nr + p if p < nr else col_start + p - nr
        own_levels[p] = jnp.transpose(jnp.broadcast_to(levels[pl.ds(g, 1), :], (128, bs)))
    pl.semaphore_wait(barrier, 6)

    parts = CHAIN // nr
    part = bs // parts

    def block_row(j):
        return j // parts * 2 % 3

    def chunk_rows(j):
        return pl.ds(pl.multiple_of(j % parts * part, part), part)

    def piece(ref, base, j):
        return ref.at[base + block_row(j), :, chunk_rows(j)]

    def swap_copy(j):
        return remote(SWAP + j, SWAP + j, piece(coupling, 0, j), piece(craw, nr * lo, j), swap)

    def relay_copy(j):
        got = piece(craw, nr * (1 - lo), j)
        return remote(RELAY + j, SWAP + j, got, got, sibling)

    def ring_copy(j, start):
        target = piece(rraw, 0, j)
        return remote(RING + j, RING + j, piece(craw, nr * core, j) if start else target, target, after)

    give_tiles = [
        [
            remote(IN + 3 * m + r, IN + 3 * m + r, density.at[give + m, rows(r)], dext.at[m, rows(r + 1), mine], pair)
            for r in range(3)
        ]
        for m in range(2)
    ]

    halo, chalo = [], []
    for m in range(2):
        moves = (
            (density.at[keep + m, rows(0)], dext.at[m, below, mine], up),
            (density.at[keep + m, rows(nr - 1)], dext.at[m, above, mine], down),
            (dext.at[m, first, other], dext.at[m, below, other], up),
            (dext.at[m, last, other], dext.at[m, above, other], down),
            (dext.at[m, inner, lcol], dext.at[m, inner, rhalo], left),
            (dext.at[m, inner, rcol], dext.at[m, inner, lhalo], right),
        )
        halo.append([remote(DHALO + 6 * m + n, DHALO + 6 * m + n, *move) for n, move in enumerate(moves)])
        moves = (
            (cext.at[m, first, across], cext.at[m, below, across], up),
            (cext.at[m, last, across], cext.at[m, above, across], down),
            (cext.at[m, inner, lcol], cext.at[m, inner, rhalo], left),
            (cext.at[m, inner, rcol], cext.at[m, inner, lhalo], right),
        )
        chalo.append([remote(CHALO + 4 * m + n, CHALO + 4 * m + n, *move) for n, move in enumerate(moves)])

    def order_chunk(raw, p, g, q, operator, weighted, at):
        held = [raw[p, s, at].astype(F32) for s in range(slots)]
        mine_levels = jnp.concatenate([own_levels[q, at]] * (bs // 128), axis=1)
        for n in range(3):
            there = levels[pl.ds((g + total + n - 1) % total, 1), :]
            x = mine_levels - there
            u = jnp.exp(jnp.abs(x) * -0.25)
            v = u * u
            v = v * v
            spectral = jnp.where(x >= 0, 1.0, v) / (1.0 + v) * u
            block = None
            for s in range(slots):
                used = (block_cols[g, s] == g + n - 1) & (s < block_count[g])
                term = held[s] * used.astype(jnp.int32).astype(F32)
                block = term if block is None else block + term
            operator[p, at, pl.ds(n * bs, bs)] = block.astype(BF)
            weighted[p, at, pl.ds(n * bs, bs)] = (block * spectral).astype(BF)

    def order_col(half, j):
        p = half * nr + block_row(j)
        order_chunk(craw, p, col_start + p, nr + p, ocol, wcol, chunk_rows(j))

    def order_row(j):
        p = block_row(j)
        order_chunk(rraw, p, k * nr + p, p, orow, wrow, chunk_rows(j))

    def taken(r, next_halo):
        give_tiles[0][r].wait_recv()
        for n in next_halo:
            halo[0][n].start()

    def due(j, at):
        return (j == at) | ((j == 0) & (at < 0)) | ((j == CHAIN) & (at > CHAIN))

    near = dist < nz // 2
    ready_source = source & (core == lo)

    def first_taken():
        halo[0][0].start()
        halo[0][1].start()
        taken(0, (2,))

    def relay_step(i, carry):
        @pl.when(i == CHAIN // 4)
        def _():
            first_taken()

        swap_copy(2 * i + core).wait_recv()
        relay_copy(2 * i + core).start()
        order_col(lo, 2 * i)
        order_col(lo, 2 * i + 1)
        return carry

    def step(j, carry):
        @pl.when(near & due(j, 12 - 5 * dist))
        def _():
            first_taken()

        @pl.when(due(j, 28 - 5 * dist))
        def _():
            taken(2, (3,))

        @pl.when(due(j, 44 - 5 * dist))
        def _():
            own_tiles[0].wait()
            taken(1, (4, 5))
            halo[1][0].start()
            halo[1][1].start()

        @pl.when(j < CHAIN)
        def _():
            @pl.when(ready_source)
            def _():
                ring_copy(j, True).start()

            @pl.when((near & (j % 2 == core)) | (jnp.logical_not(ready_source) & (j % 2 != core)))
            def _():
                swap_copy(j).wait_recv()

            @pl.when(near & (j % 2 == core))
            def _():
                relay_copy(j).start()

            @pl.when(source & (core != lo))
            def _():
                ring_copy(j, True).start()

            @pl.when(jnp.logical_not(ready_source))
            def _():
                order_col(1 - lo, j)

            @pl.when(dist != 0)
            def _():
                ring_copy(j, False).wait_recv()

            @pl.when((dist != 0) & (dist < nz - 1))
            def _():
                ring_copy(j, False).start()

            @pl.when(dist != 0)
            def _():
                order_row(j)

        return carry

    for i in range(CHAIN // 2):
        swap_copy(2 * i + core).start()
    for m in range(2):
        for r in ORDER:
            give_tiles[m][r].start()
    own_cols.wait()

    @pl.when(jnp.logical_not(near))
    def _():
        lax.fori_loop(0, CHAIN // 2, relay_step, 0)

    lax.fori_loop(0, CHAIN + 1, step, 0)

    @pl.when(near)
    def _():
        def own_col_step(j, carry):
            order_col(lo, j)
            return carry

        lax.fori_loop(0, CHAIN, own_col_step, 0)

    @pl.when(ready_source)
    def _():
        def other_col_step(j, carry):
            @pl.when(j % 2 != core)
            def _():
                swap_copy(j).wait_recv()

            order_col(1 - lo, j)
            return carry

        lax.fori_loop(0, CHAIN, other_col_step, 0)

    @pl.when(source)
    def _():
        own_rows.start()
        own_rows.wait()

        def own_step(j, carry):
            order_row(j)
            return carry

        lax.fori_loop(0, CHAIN, own_step, 0)

    def blocks(m, i, h, c, count, source_ref, row_op, col_op, store):
        base = pl.multiple_of((h * nr + c) * bs, bs)
        through_rows = jnp.dot(
            row_op[i], source_ref[m, pl.ds(i * bs, 3 * bs), pl.ds(pl.multiple_of(base + bs, bs), count * bs)],
            preferred_element_type=F32,
        )
        for j in range(count):
            through_cols = lax.dot_general(
                source_ref[m, rows(i + 1), pl.ds(pl.multiple_of(base + j * bs, bs), 3 * bs)], col_op[h * nr + c + j],
                (((1,), (1,)), ((), ())), preferred_element_type=F32,
            )
            store(j, through_rows[:, j * bs : (j + 1) * bs], through_cols)

    def commutand_row(m, i):
        def half(h, carry):
            def store(j, through_rows, through_cols):
                at = pl.multiple_of(h * tile + (j + 1) * bs, bs)
                cext[m, rows(i + 1), pl.ds(at, bs)] = (through_rows - through_cols).astype(BF)

            blocks(m, i, h, 0, nr, dext, wrow, wcol, store)
            return carry

        lax.fori_loop(0, 2, half, 0)

    inside, edge = pl.ds(pl.multiple_of(lo * bs, bs), 2 * bs), pl.ds(pl.multiple_of(2 * (1 - lo) * bs, bs), bs)
    back = [
        [
            [
                remote(OUT + n, OUT + n, res.at[m, rows(i), where], out.at[keep + m, rows(i), where], pair)
                for n, where in ((6 * m + 2 * i, inside), (6 * m + 2 * i + 1, edge))
            ]
            for i in range(3)
        ]
        for m in range(2)
    ]

    def to_pair(m, i, at_edge):
        start = 2 * (1 - lo) if at_edge else lo

        def store(j, through_rows, through_cols):
            at = pl.multiple_of((start + j) * bs, bs)
            res[m, rows(i), pl.ds(at, bs)] = (through_cols - through_rows).astype(BF)

        blocks(m, i, 1 - lo, start, 1 if at_edge else 2, cext, orow, ocol, store)
        back[m][i][at_edge].start()

    def to_own(m, i):
        def store(j, through_rows, through_cols):
            out[keep + m, rows(i), rows(j)] = (through_cols - through_rows).astype(BF)

        blocks(m, i, lo, 0, nr, cext, orow, ocol, store)

    def row_to_pair(m, i):
        to_pair(m, i, 0)
        to_pair(m, i, 1)

    def give_on(r, which):
        give_tiles[1][r].wait_recv()
        for n in which:
            halo[1][n].start()

    for copy in halo[0]:
        copy.wait_recv()
    commutand_row(0, 0)
    chalo[0][0].start()
    commutand_row(0, 2)
    chalo[0][1].start()
    commutand_row(0, 1)
    chalo[0][2].start()
    chalo[0][3].start()
    give_on(0, (2,))
    give_on(2, (3,))
    to_pair(0, 1, 0)
    own_tiles[1].wait()
    give_on(1, (4, 5))
    chalo[0][2].wait_recv()
    chalo[0][3].wait_recv()
    to_pair(0, 1, 1)
    to_own(0, 1)
    chalo[0][1].wait_recv()
    row_to_pair(0, 0)
    for copy in halo[1]:
        copy.wait_recv()
    commutand_row(1, 0)
    chalo[1][0].start()
    chalo[0][0].wait_recv()
    row_to_pair(0, 2)
    commutand_row(1, 2)
    chalo[1][1].start()
    commutand_row(1, 1)
    chalo[1][2].start()
    chalo[1][3].start()
    to_pair(1, 1, 0)
    to_own(0, 0)
    to_own(0, 2)
    chalo[1][2].wait_recv()
    chalo[1][3].wait_recv()
    to_pair(1, 1, 1)
    to_own(1, 1)
    chalo[1][1].wait_recv()
    row_to_pair(1, 0)
    chalo[1][0].wait_recv()
    row_to_pair(1, 2)
    to_own(1, 0)
    to_own(1, 2)

    for i in range(CHAIN // 2):
        swap_copy(2 * i + core).wait_send()
        relay_copy(2 * i + core).wait_send()
    for j in range(CHAIN):

        @pl.when(dist < nz - 1)
        def _():
            ring_copy(j, False).wait_send()

    for r in range(3):
        give_tiles[0][r].wait_send()
        give_tiles[1][r].wait_send()
    for m in range(2):
        for copy in halo[m] + chalo[m]:
            copy.wait_send()
        for i in range(3):
            for copy in back[m][i]:
                copy.wait_send()
                copy.wait_recv()


def body(density, coupling, block_cols, block_count, energies):
    copies, halves, tile, _ = density.shape
    nr, slots, bs, _ = coupling.shape
    nk, nb = lax.axis_size("ket"), lax.axis_size("bra")
    total = block_cols.shape[0]
    any_space = pl.BlockSpec(memory_space=pl.ANY)
    vmem = pl.BlockSpec(memory_space=pltpu.VMEM)
    smem = pl.BlockSpec(memory_space=pltpu.SMEM)
    out = pl.pallas_call(
        functools.partial(kernel, nk, nb),
        out_shape=pltpu.VMEM((copies * halves, tile, tile), density.dtype),
        in_specs=[any_space, any_space, vmem, smem, smem],
        out_specs=vmem,
        scratch_shapes=[
            pltpu.VMEM((2, tile + 2 * bs, 2 * tile + 2 * bs), BF),
            pltpu.VMEM((2, tile + 2 * bs, 2 * tile + 2 * bs), BF),
            pltpu.VMEM((2, tile, tile), BF),
            pltpu.VMEM((nr, slots, bs, bs), BF),
            pltpu.VMEM((2 * nr, slots, bs, bs), BF),
            pltpu.VMEM((nr, bs, 3 * bs), BF),
            pltpu.VMEM((2 * nr, bs, 3 * bs), BF),
            pltpu.VMEM((nr, bs, 3 * bs), BF),
            pltpu.VMEM((2 * nr, bs, 3 * bs), BF),
            pltpu.VMEM((3 * nr, bs, 128), F32),
            pltpu.SemaphoreType.DMA((COPIES,)),
            pltpu.SemaphoreType.DMA((COPIES,)),
            pltpu.SemaphoreType.DMA((4,)),
        ],
        compiler_params=pltpu.CompilerParams(
            collective_id=0, has_side_effects=True, vmem_limit_bytes=52 << 20
        ),
        name="dissipator",
    )(density.reshape(copies * halves, tile, tile), coupling, energies.reshape(total, bs), block_cols, block_count)
    return out.reshape(density.shape)


def solution(mesh):
    return jax.shard_map(
        body,
        mesh=mesh,
        in_specs=(P(None, None, "ket", "bra"), P("bra", None, None, None), P(), P(), P()),
        out_specs=P(None, None, "ket", "bra"),
        check_vma=False,
    )
```

time: 149 us -> 134 us (0.90)
  Pallas kernels: 143 us -> 129 us
    pallas_call x1, Pallas kernels: 143 us -> 129 us  [body(): pl.pallas_call(functools.partial(kernel, nk, nb), out_shape=pltpu.VMEM((c...]
where the time goes in v3:
time: 134 us
  Pallas kernels  129 us (96%)
  local copies, waits for them, and re-layouts  4.98 us (4%)
    pallas_call x1, Pallas kernels, body(): pl.pallas_call(functools.partial(kernel, nk, nb), out_shape=pltpu.VMEM((c...  129 us
    unnamed x2, local copies, waits for them, and re-layouts  3.55 us

profile of v3, /device:TPU:16, one launch (start us, length us, event | category | flops | bytes accessed | tf_op | source)
XLA Modules:
  0.0 133.5 jit_solution(18045321264141393629)
XLA Ops:
  0.0 1.4 %copy.6.block_cols = s32[48,3]{1,0:T(8,128)} copy(s32[48,3]{0,1:T(4,128)} %param.7) | data formatting | bytes 1152 | tf_op args[2]
  1.4 1.4 %reshape.10.levels = f32[48,256]{1,0:T(8,128)} reshape(f32[12288]{0:T(1024)} %param.9) | data formatting | bytes 98304 | tf_op jit(solution)/shard_map/reshape | solution.py:444
  2.8 128.5 %dissipator.1 = bf16[4,768,768]{2,1,0:T(8,128)(2,1)S(1)} custom-call(bf16[4,768,768]{2,1,0:T(8,128)(2,1)} %bitcast.3, bf16[3,3,256,256]{3,2,1,0:T(8,128)(2,1)} %coupling.1, f32[48,256]{1,0:T(8,128)} %reshape.10.levels, s32[48,3]{1,0:T(8,128)} %copy.6.block_cols, s32[48]{0:T(128)} %block_count.1), custom_call_target="tpu_custom_call" | custom-call | tf_op jit(solution)/shard_map/dissipator/pallas_call | solution.py:420
  131.3 2.2 %copy.8 = bf16[2,2,768,768]{3,2,1,0:T(8,128)(2,1)} copy(bf16[2,2,768,768]{3,2,1,0:T(8,128)(2,1)S(1)} %bitcast.2) | data formatting | bytes 9437184

commit v4 on v3

--- a/solution.py
+++ b/solution.py
@@ -28,7 +28,7 @@
 ):
     nr, slots, bs, _ = coupling.shape
     tile = nr * bs
-    total = block_cols.shape[0]
+    total = block_cols.shape[1]
     k, b = lax.axis_index("ket"), lax.axis_index("bra")
     core, hi, lo, z, nz = k % 2, (k // 2) % 2, b % 2, b // 2, nb // 2
     flip = b + 1 - 2 * lo
@@ -77,10 +77,14 @@
     for device in (pair, swap, up, down, left, right):
         pl.semaphore_signal(barrier, inc=1, device_id=device, device_id_type=MESH)
 
+    def level_row(g):
+        count = bs // 128
+        return jnp.concatenate([levels[pl.ds(g * count + n, 1), :] for n in range(count)], axis=1)
+
     col_start = b // 2 * 2 * nr
     for p in range(3 * nr):
         g = k * nr + p if p < nr else col_start + p - nr
-        own_levels[p] = jnp.transpose(jnp.broadcast_to(levels[pl.ds(g, 1), :], (128, bs)))
+        own_levels[p] = jnp.transpose(jnp.broadcast_to(level_row(g), (128, bs)))
     pl.semaphore_wait(barrier, 6)
 
     parts = CHAIN // nr
@@ -137,7 +141,7 @@
         held = [raw[p, s, at].astype(F32) for s in range(slots)]
         mine_levels = jnp.concatenate([own_levels[q, at]] * (bs // 128), axis=1)
         for n in range(3):
-            there = levels[pl.ds((g + total + n - 1) % total, 1), :]
+            there = level_row((g + total + n - 1) % total)
             x = mine_levels - there
             u = jnp.exp(jnp.abs(x) * -0.25)
             v = u * u
@@ -145,7 +149,7 @@
             spectral = jnp.where(x >= 0, 1.0, v) / (1.0 + v) * u
             block = None
             for s in range(slots):
-                used = (block_cols[g, s] == g + n - 1) & (s < block_count[g])
+                used = (block_cols[s, g] == g + n - 1) & (s < block_count[g])
                 term = held[s] * used.astype(jnp.int32).astype(F32)
                 block = term if block is None else block + term
             operator[p, at, pl.ds(n * bs, bs)] = block.astype(BF)
@@ -441,7 +445,7 @@
             collective_id=0, has_side_effects=True, vmem_limit_bytes=52 << 20
         ),
         name="dissipator",
-    )(density.reshape(copies * halves, tile, tile), coupling, energies.reshape(total, bs), block_cols, block_count)
+    )(density.reshape(copies * halves, tile, tile), coupling, energies.reshape(total * bs // 128, 128), block_cols.T, block_count)
     return out.reshape(density.shape)
 
 

time: 134 us -> 130 us (0.970)
  local copies, waits for them, and re-layouts: 4.98 us -> 2.19 us
    reshape x1 -> x0, local copies, waits for them, and re-layouts: 1.43 us -> none  [body(): energies.reshape(total, bs)]
    unnamed x2 -> x1, local copies, waits for them, and re-layouts: 3.55 us -> 2.19 us
where the time goes in v4:
time: 130 us
  Pallas kernels  128 us (98%)
  local copies, waits for them, and re-layouts  2.19 us (2%)
    pallas_call x1, Pallas kernels, body(): pl.pallas_call(functools.partial(kernel, nk, nb), out_shape=pltpu.VMEM((c...  128 us

profile of v4, /device:TPU:16, one launch (start us, length us, event | category | flops | bytes accessed | tf_op | source)
XLA Modules:
  0.0 130.3 jit_solution(11688724602155777686)
XLA Ops:
  0.0 128.1 %dissipator.1 = bf16[4,768,768]{2,1,0:T(8,128)(2,1)S(1)} custom-call(bf16[4,768,768]{2,1,0:T(8,128)(2,1)} %bitcast.5, bf16[3,3,256,256]{3,2,1,0:T(8,128)(2,1)} %coupling.1, f32[96,128]{1,0:T(8,128)} %bitcast.6, s32[3,48]{1,0:T(4,128)} %bitcast.7, s32[48]{0:T(128)} %block_count.1), custom_call_target="tpu_custom_call" | custom-call | tf_op jit(solution)/shard_map/dissipator/pallas_call | solution.py:424
  128.1 2.2 %copy.7 = bf16[2,2,768,768]{3,2,1,0:T(8,128)(2,1)} copy(bf16[2,2,768,768]{3,2,1,0:T(8,128)(2,1)S(1)} %bitcast.4) | data formatting | bytes 9437184

commit v5 on v4

--- a/solution.py
+++ b/solution.py
@@ -347,20 +347,20 @@
         for n in which:
             halo[1][n].start()
 
+    give_on(0, (2,))
+    give_on(2, (3,))
     for copy in halo[0]:
         copy.wait_recv()
     commutand_row(0, 0)
     chalo[0][0].start()
     commutand_row(0, 2)
     chalo[0][1].start()
+    own_tiles[1].wait()
+    give_on(1, (4, 5))
     commutand_row(0, 1)
     chalo[0][2].start()
     chalo[0][3].start()
-    give_on(0, (2,))
-    give_on(2, (3,))
     to_pair(0, 1, 0)
-    own_tiles[1].wait()
-    give_on(1, (4, 5))
     chalo[0][2].wait_recv()
     chalo[0][3].wait_recv()
     to_pair(0, 1, 1)

time: 130 us -> 130 us (level); the launches traced: 130 us -> 129 us
  Pallas kernels: 128 us -> 126 us
    pallas_call x1, Pallas kernels: 128 us -> 126 us  [body(): pl.pallas_call(functools.partial(kernel, nk, nb), out_shape=pltpu.VMEM((c...]
where the time goes in v5:
time: 130 us; the launch traced here: 129 us
  Pallas kernels  126 us (97%)
  local copies, waits for them, and re-layouts  2.19 us (2%)
    pallas_call x1, Pallas kernels, body(): pl.pallas_call(functools.partial(kernel, nk, nb), out_shape=pltpu.VMEM((c...  126 us

profile of v5, /device:TPU:16, one launch (start us, length us, event | category | flops | bytes accessed | tf_op | source)
XLA Modules:
  0.0 128.7 jit_solution(2064248589701114067)
XLA Ops:
  0.0 126.5 %dissipator.1 = bf16[4,768,768]{2,1,0:T(8,128)(2,1)S(1)} custom-call(bf16[4,768,768]{2,1,0:T(8,128)(2,1)} %bitcast.5, bf16[3,3,256,256]{3,2,1,0:T(8,128)(2,1)} %coupling.1, f32[96,128]{1,0:T(8,128)} %bitcast.6, s32[3,48]{1,0:T(4,128)} %bitcast.7, s32[48]{0:T(128)} %block_count.1), custom_call_target="tpu_custom_call" | custom-call | tf_op jit(solution)/shard_map/dissipator/pallas_call | solution.py:424
  126.5 2.2 %copy.7 = bf16[2,2,768,768]{3,2,1,0:T(8,128)(2,1)} copy(bf16[2,2,768,768]{3,2,1,0:T(8,128)(2,1)S(1)} %bitcast.4) | data formatting | bytes 9437184
